TPU v7x, 32 devices: a whole 2x2x4 slice. The times are simulated.
32 devices in a mesh: section: 4 (over x, core), dp: 8 (over z, y).
Axes of the slice: x: 2, y: 2, z: 4, core: 2. Of those that a mesh axis runs over, the one named last changes fastest.
Arguments:
- section_inputs: bfloat16 [4, 4, 1024, 2048], P('section', None, 'dp'), may hold values from -8 to 8
- top_grads: bfloat16 [4, 1024, 2048], P(None, 'dp'), may hold values from -8 to 8
- query_weight: bfloat16 [4, 2048, 1024], P('section'), may hold values from -0.375 to 0.375
- output_weight: bfloat16 [4, 2048, 1024], P('section'), may hold values from -0.125 to 0.125
- neighbour_kv: bfloat16 [4, 16, 2, 128, 1024], P('section', 'dp'), may hold values from -6 to 6
- nbr_ids: int32 [4, 16, 2], P(None, 'dp'), may hold values from 0 to 15, as said below
- send_list: int32 [8, 8], replicated, may hold values from 0 to 1, as said below
- send_counts: int32 [8, 8], replicated, may hold values from 0 to 1, as said below
Outputs:
- input_grads: bfloat16 [4, 4, 1024, 2048], P('section', None, 'dp')
- query_grads: bfloat16 [4, 2048, 1024], P('section', 'dp')
- output_grads: bfloat16 [4, 2048, 1024], P('section', 'dp')
- kv_grads: bfloat16 [4, 16, 2, 128, 1024], P('section', 'dp')
Inputs may be any that keep to these rules, and one draw needn't show every extreme that they name: `nbr_ids`: the 2 neighbours of a span have different owners. Every neighbour of reader r's spans owned by o is block o * 2 + send_list[o, r]. `send_list`: entry [o, r] is 0 where send_counts[o, r] is 0. `send_counts`: entry [o, r] is 1 where some span of reader r has a neighbour of owner o, else 0.
All inputs are finite; a program needn't handle non-finite values.
Results may differ from a plain program's by a relative error of at most 0.039.
Values may be sent and summed in bfloat16 or wider, within the bound.
No kernel may reach another device: no remote copies, remote signals or barrier semaphores. Data moves between devices by JAX's collectives and lax.ppermute only.
A program may use at most 192 MiB of HBM per device.

v0:
```python
import jax
import jax.numpy as jnp
from jax import lax
from jax.sharding import PartitionSpec as P

HEADS = 16
HEAD_DIM = 64
SPAN = 64
K_NBR = 2
NBR_LEN = 128


highest = lax.Precision.HIGHEST


def from_behind(x, axis, by):
    size = lax.axis_size(axis)
    pairs = [(i, i + by) for i in range(size) if 0 <= i + by < size]
    return lax.ppermute(x, axis, pairs)


def transposed_product(left, right):
    return lax.dot_general(
        left, right, (((0,), (0,)), ((), ())), preferred_element_type=jnp.float32
    )


def right_transposed(left, right):
    return lax.dot_general(
        left, right, (((1,), (1,)), ((), ())), preferred_element_type=jnp.float32
    )


def section_backward(inputs, upstream, owner_ids, fetched, query_proj, output_proj):
    tokens, model_width = inputs.shape
    inner_width = query_proj.shape[1]
    spans = tokens // SPAN
    score_scale = HEAD_DIM ** (-0.5)
    ref_owner = owner_ids.reshape(-1)
    blocks = jnp.take(fetched, ref_owner, axis=0)
    blocks = blocks.reshape(spans, K_NBR, 2, NBR_LEN, HEADS, HEAD_DIM)
    key_rows = blocks[:, :, 0].reshape(spans, K_NBR * NBR_LEN, HEADS, HEAD_DIM)
    value_rows = blocks[:, :, 1].reshape(spans, K_NBR * NBR_LEN, HEADS, HEAD_DIM)
    query_rows = jnp.dot(inputs, query_proj, preferred_element_type=jnp.float32).astype(
        jnp.bfloat16
    )
    heads_q = query_rows.reshape(spans, SPAN, HEADS, HEAD_DIM)
    scores = (
        jnp.einsum("cqhd,ckhd->chqk", heads_q, key_rows, preferred_element_type=jnp.float32)
        * score_scale
    )
    weights = jnp.exp(scores - jnp.max(scores, axis=-1, keepdims=True))
    probability = weights / jnp.sum(weights, axis=-1, keepdims=True)
    prob_rounded = probability.astype(jnp.bfloat16)
    attended = jnp.einsum(
        "chqk,ckhd->cqhd", prob_rounded, value_rows, preferred_element_type=jnp.float32
    )
    attended = attended.astype(jnp.bfloat16).reshape(tokens, inner_width)
    d_attended = jnp.dot(upstream, output_proj, preferred_element_type=jnp.float32).astype(
        jnp.bfloat16
    )
    heads_d = d_attended.reshape(spans, SPAN, HEADS, HEAD_DIM)
    d_probs = jnp.einsum("cqhd,ckhd->chqk", heads_d, value_rows, preferred_element_type=jnp.float32)
    row_delta = jnp.sum(probability * d_probs, axis=-1, keepdims=True)
    d_scores = (probability * (d_probs - row_delta) * score_scale).astype(jnp.bfloat16)
    d_query = jnp.einsum("chqk,ckhd->cqhd", d_scores, key_rows, preferred_element_type=jnp.float32)
    d_query = d_query.astype(jnp.bfloat16).reshape(tokens, inner_width)
    d_keys = jnp.einsum("chqk,cqhd->ckhd", d_scores, heads_q, preferred_element_type=jnp.float32)
    d_values = jnp.einsum(
        "chqk,cqhd->ckhd", prob_rounded, heads_d, preferred_element_type=jnp.float32
    )
    per_ref = jnp.stack(
        [
            d_keys.reshape(spans * K_NBR, NBR_LEN * inner_width),
            d_values.reshape(spans * K_NBR, NBR_LEN * inner_width),
        ],
        axis=1,
    )
    per_ref = per_ref.reshape(spans * K_NBR, 2 * NBR_LEN * inner_width)
    grads_in = (upstream.astype(jnp.float32) + right_transposed(d_query, query_proj)).astype(
        jnp.bfloat16
    )
    return (grads_in, d_query, attended, per_ref)


def body(
    section_inputs,
    top_grads,
    query_weight,
    output_weight,
    neighbour_kv,
    nbr_ids,
    send_list,
    send_counts,
):
    n_section = lax.axis_size("section")
    section_index = lax.axis_index("section")
    n_data = lax.axis_size("dp")
    data_index = lax.axis_index("dp")
    inputs_all = section_inputs[0]
    query_proj = query_weight[0]
    output_proj = output_weight[0]
    owned_blocks = neighbour_kv[0]
    micro_count, tok_dev, model_width = inputs_all.shape
    blk_dev = owned_blocks.shape[0]
    inner_width = query_proj.shape[1]
    owned_flat = owned_blocks.reshape(blk_dev, -1)
    flat_size = owned_flat.shape[1]
    ref_count = tok_dev // SPAN * K_NBR
    owner_range = jnp.arange(n_data, dtype=jnp.int32)
    my_list = lax.dynamic_index_in_dim(send_list, data_index, 0, keepdims=False)
    my_counts = lax.dynamic_index_in_dim(send_counts, data_index, 0, keepdims=False)
    outbound = (
        (my_list[:, None] == jnp.arange(blk_dev, dtype=jnp.int32)[None, :])
        & (my_counts[:, None] > 0)
    ).astype(jnp.bfloat16)
    whole_pool = lax.all_gather(owned_flat, "dp", axis=0, tiled=True)
    column_list = lax.dynamic_index_in_dim(send_list, data_index, 1, keepdims=False)
    column_counts = lax.dynamic_index_in_dim(send_counts, data_index, 1, keepdims=False)
    target = owner_range * blk_dev + column_list
    inbound = (
        (target[:, None] == jnp.arange(n_data * blk_dev, dtype=jnp.int32)[None, :])
        & (column_counts[:, None] > 0)
    ).astype(jnp.bfloat16)
    fetched = jnp.dot(inbound, whole_pool, preferred_element_type=jnp.float32).astype(jnp.bfloat16)
    tick_count = n_section + micro_count - 1
    section_lag = n_section - 1 - section_index
    last_section = section_index == n_section - 1

    def run_tick(tick_index, loop_state):
        arriving, grads_store, query_store, attended_store, upstream_store, ref_store = loop_state
        micro_now = tick_index - section_lag
        is_valid = (micro_now >= 0) & (micro_now < micro_count)
        slot_index = jnp.clip(micro_now, 0, micro_count - 1)
        inputs = lax.dynamic_index_in_dim(inputs_all, slot_index, 0, keepdims=False)
        top_rows = lax.dynamic_index_in_dim(top_grads, slot_index, 0, keepdims=False)
        upstream = jnp.where(last_section, top_rows, arriving)
        owner_ids = lax.dynamic_index_in_dim(nbr_ids, slot_index, 0, keepdims=False) // blk_dev
        grads_in, d_query, attended, per_ref = section_backward(
            inputs, upstream, owner_ids, fetched, query_proj, output_proj
        )

        def place_row(store, value):
            previous = lax.dynamic_index_in_dim(store, slot_index, 0, keepdims=False)
            return lax.dynamic_update_index_in_dim(
                store, jnp.where(is_valid, value, previous), slot_index, 0
            )

        grads_store = place_row(grads_store, grads_in)
        query_store = place_row(query_store, d_query)
        attended_store = place_row(attended_store, attended)
        upstream_store = place_row(upstream_store, upstream)
        ref_store = place_row(ref_store, per_ref)
        leaving = jnp.where(is_valid, grads_in, jnp.zeros_like(grads_in))
        arriving = from_behind(leaving, "section", -1)
        return (arriving, grads_store, query_store, attended_store, upstream_store, ref_store)

    initial = (
        jnp.zeros((tok_dev, model_width), jnp.bfloat16),
        jnp.zeros((micro_count, tok_dev, model_width), jnp.bfloat16),
        jnp.zeros((micro_count, tok_dev, inner_width), jnp.bfloat16),
        jnp.zeros((micro_count, tok_dev, inner_width), jnp.bfloat16),
        jnp.zeros((micro_count, tok_dev, model_width), jnp.bfloat16),
        jnp.zeros((micro_count, ref_count, flat_size), jnp.float32),
    )
    final_state = lax.fori_loop(0, tick_count, run_tick, initial)
    arriving, grads_store, query_store, attended_store, upstream_store, ref_store = final_state
    owner_all = (nbr_ids // blk_dev).reshape(-1)
    selector_all = (owner_all[:, None] == owner_range[None, :]).astype(jnp.float32)
    partial_sum = lax.dot_general(
        selector_all,
        ref_store.reshape(micro_count * ref_count, flat_size),
        (((0,), (0,)), ((), ())),
        precision=highest,
        preferred_element_type=jnp.float32,
    )
    input_rows = inputs_all.reshape(micro_count * tok_dev, model_width)
    upstream_rows = upstream_store.reshape(micro_count * tok_dev, model_width)
    query_rows = query_store.reshape(micro_count * tok_dev, inner_width)
    attended_rows = attended_store.reshape(micro_count * tok_dev, inner_width)
    grad_scale = (micro_count * tok_dev * n_data) ** (-0.5)
    query_term = transposed_product(input_rows, query_rows)
    output_term = transposed_product(upstream_rows, attended_rows)
    shares = lax.psum_scatter(
        (jnp.concatenate([query_term, output_term], axis=1) * grad_scale).astype(jnp.bfloat16),
        "dp",
        scatter_dimension=0,
        tiled=True,
    ).astype(jnp.float32)
    query_grads = shares[:, :inner_width].astype(jnp.bfloat16)
    output_grads = shares[:, inner_width:].astype(jnp.bfloat16)
    returning = lax.all_to_all(
        partial_sum.astype(jnp.bfloat16), "dp", split_axis=0, concat_axis=0, tiled=True
    )
    block_grads = transposed_product(outbound, returning).astype(jnp.bfloat16)
    return (
        grads_store[None],
        query_grads[None],
        output_grads[None],
        block_grads.reshape(owned_blocks.shape)[None],
    )


def solution(mesh):
    in_specs = (
        P("section", None, "dp", None),
        P(None, "dp", None),
        P("section", None, None),
        P("section", None, None),
        P("section", "dp", None, None, None),
        P(None, "dp", None),
        P(),
        P(),
    )
    out_specs = (
        P("section", None, "dp", None),
        P("section", "dp", None),
        P("section", "dp", None),
        P("section", "dp", None, None, None),
    )
    return jax.shard_map(body, mesh=mesh, in_specs=in_specs, out_specs=out_specs, check_vma=False)
```

profile of v0, /device:TPU:9, one launch (start us, length us, event | category | flops | bytes accessed | tf_op | source)
XLA Modules:
  0.0 1403.7 jit_solution(17649420041519584705)
XLA Ops:
  10.8 123.8 %all-gather.3.cloned.1.call-done = bf16[8,2,262144]{2,1,0:T(2,128)(2,1)} async-done(((bf16[1,2,262144]{2,1,0:T(2,128)(2,1)}), bf16[8,2,262144]{2,1,0:T(2,128)(2,1)}) %all-gather.3.cloned.1.call-update) | async-done | bytes 8388624 | tf_op jit(solution)/shard_map/all_gather | solution.py:117
  134.6 7.3 reshape.270
  141.9 6.6 convolution_convert_fusion.4
  154.8 6.0 broadcast_in_dim.76
  160.8 1005.1 %while.25 = (s32[]{:T(128)}, bf16[128,2048]{1,0:T(8,128)(2,1)}, bf16[4,128,2048]{2,1,0:T(8,128)(2,1)}, bf16[4,128,1024]{2,1,0:T(8,128)(2,1)}, bf16[4,128,1024]{2...) while((s32[]{:T(128)}, bf16[128,2048]{1,0:T(8,128)(2,1)}, ...), condition=%wide.region_4.5_spmd, body=%wide.region_0.4_spmd.sunk | while | flops 2036340736 | bytes 156718256 | solution.py:166
  165.7 4.1 gather_fusion
  172.3 18.7 %pad_maximum_fusion.4 = bf16[4,262144]{1,0:T(4,128)(2,1)} fusion(bf16[4,87296]{1,0:T(4,128)(2,1)S(1)} %copy-done.2, bf16[4,87424]{1,0:T(4,128)(2,1)S(1)} %gather_fusion.1, bf16[4,87424]{1,0:T(4,128)(2,1)S(1)} %gather_fusion.2), kind=kLoop, calls=%fused_computation.10.clone.1 | loop fusion | flops 6291456 | bytes 4194304 | tf_op jit(solution)/shard_map/while
  229.7 15.4 %fusion.121 = bf16[2,64,16,64]{1,3,2,0:T(8,128)(2,1)} fusion(bf16[2,256,16,64]{1,3,2,0:T(8,128)(2,1)S(1)} %copy-done, f32[2,16,64,256]{3,2,1,0:T(8,128)} %fusion.119, f32[2,16,64,256]{3,2,1,0:T(8,128)} %get-tuple-element.600, f32[2,16,64]{2,1,0:T(8,128)S(1)} %get-tuple-element.601), kind=kOutput, calls=%fused_computation.23.clone.1 | convolution fusion | flops 70912256 | bytes 5513216 | tf_op jit(solution)/shard_map/while/body/eval_jaxpr/chqk,ckhd->cqhd/dot_general | solution.py:66
  247.0 4.8 broadcast_select_fusion.5
  258.9 16.0 %convolution_bitcast_fusion.7 = f32[2,256,16,64]{1,3,2,0:T(8,128)} fusion(bf16[2,64,16,64]{1,3,2,0:T(8,128)(2,1)S(1)} %copy-done.4, f32[2,16,64,256]{3,2,1,0:T(8,128)} %fusion.119, f32[2,16,64,256]{3,2,1,0:T(8,128)} %get-tuple-element.600, f32[2,16,64]{2,1,0:T(8,128)S(1)} %get-tuple-element.601), kind=kOutput, calls=%fused_computation.18.clone.1 | convolution fusion | flops 70781184 | bytes 6561792 | tf_op jit(solution)/shard_map/while/body/eval_jaxpr/chqk,cqhd->ckhd/dot_general | solution.py:68
  283.4 4.9 copy.97
  288.3 5.2 reshape.306
  309.1 4.1 gather_fusion
  315.7 18.9 %pad_maximum_fusion.4 = bf16[4,262144]{1,0:T(4,128)(2,1)} fusion(bf16[4,87296]{1,0:T(4,128)(2,1)S(1)} %copy-done.2, bf16[4,87424]{1,0:T(4,128)(2,1)S(1)} %gather_fusion.1, bf16[4,87424]{1,0:T(4,128)(2,1)S(1)} %gather_fusion.2), kind=kLoop, calls=%fused_computation.10.clone.1 | loop fusion | flops 6291456 | bytes 4194304 | tf_op jit(solution)/shard_map/while
  373.0 15.4 %fusion.121 = bf16[2,64,16,64]{1,3,2,0:T(8,128)(2,1)} fusion(bf16[2,256,16,64]{1,3,2,0:T(8,128)(2,1)S(1)} %copy-done, f32[2,16,64,256]{3,2,1,0:T(8,128)} %fusion.119, f32[2,16,64,256]{3,2,1,0:T(8,128)} %get-tuple-element.600, f32[2,16,64]{2,1,0:T(8,128)S(1)} %get-tuple-element.601), kind=kOutput, calls=%fused_computation.23.clone.1 | convolution fusion | flops 70912256 | bytes 5513216 | tf_op jit(solution)/shard_map/while/body/eval_jaxpr/chqk,ckhd->cqhd/dot_general | solution.py:66
  390.3 4.8 broadcast_select_fusion.5
  401.2 16.0 %convolution_bitcast_fusion.7 = f32[2,256,16,64]{1,3,2,0:T(8,128)} fusion(bf16[2,64,16,64]{1,3,2,0:T(8,128)(2,1)S(1)} %copy-done.4, f32[2,16,64,256]{3,2,1,0:T(8,128)} %fusion.119, f32[2,16,64,256]{3,2,1,0:T(8,128)} %get-tuple-element.600, f32[2,16,64]{2,1,0:T(8,128)S(1)} %get-tuple-element.601), kind=kOutput, calls=%fused_computation.18.clone.1 | convolution fusion | flops 70781184 | bytes 6561792 | tf_op jit(solution)/shard_map/while/body/eval_jaxpr/chqk,cqhd->ckhd/dot_general | solution.py:68
  425.7 4.9 copy.97
  430.6 5.2 reshape.306
  451.5 4.1 gather_fusion
  458.2 18.7 %pad_maximum_fusion.4 = bf16[4,262144]{1,0:T(4,128)(2,1)} fusion(bf16[4,87296]{1,0:T(4,128)(2,1)S(1)} %copy-done.2, bf16[4,87424]{1,0:T(4,128)(2,1)S(1)} %gather_fusion.1, bf16[4,87424]{1,0:T(4,128)(2,1)S(1)} %gather_fusion.2), kind=kLoop, calls=%fused_computation.10.clone.1 | loop fusion | flops 6291456 | bytes 4194304 | tf_op jit(solution)/shard_map/while
  515.3 15.4 %fusion.121 = bf16[2,64,16,64]{1,3,2,0:T(8,128)(2,1)} fusion(bf16[2,256,16,64]{1,3,2,0:T(8,128)(2,1)S(1)} %copy-done, f32[2,16,64,256]{3,2,1,0:T(8,128)} %fusion.119, f32[2,16,64,256]{3,2,1,0:T(8,128)} %get-tuple-element.600, f32[2,16,64]{2,1,0:T(8,128)S(1)} %get-tuple-element.601), kind=kOutput, calls=%fused_computation.23.clone.1 | convolution fusion | flops 70912256 | bytes 5513216 | tf_op jit(solution)/shard_map/while/body/eval_jaxpr/chqk,ckhd->cqhd/dot_general | solution.py:66
  532.5 4.8 broadcast_select_fusion.5
  543.6 16.0 %convolution_bitcast_fusion.7 = f32[2,256,16,64]{1,3,2,0:T(8,128)} fusion(bf16[2,64,16,64]{1,3,2,0:T(8,128)(2,1)S(1)} %copy-done.4, f32[2,16,64,256]{3,2,1,0:T(8,128)} %fusion.119, f32[2,16,64,256]{3,2,1,0:T(8,128)} %get-tuple-element.600, f32[2,16,64]{2,1,0:T(8,128)S(1)} %get-tuple-element.601), kind=kOutput, calls=%fused_computation.18.clone.1 | convolution fusion | flops 70781184 | bytes 6561792 | tf_op jit(solution)/shard_map/while/body/eval_jaxpr/chqk,cqhd->ckhd/dot_general | solution.py:68
  568.1 4.9 copy.97
  573.0 5.2 reshape.306
  593.7 4.1 gather_fusion
  600.4 18.7 %pad_maximum_fusion.4 = bf16[4,262144]{1,0:T(4,128)(2,1)} fusion(bf16[4,87296]{1,0:T(4,128)(2,1)S(1)} %copy-done.2, bf16[4,87424]{1,0:T(4,128)(2,1)S(1)} %gather_fusion.1, bf16[4,87424]{1,0:T(4,128)(2,1)S(1)} %gather_fusion.2), kind=kLoop, calls=%fused_computation.10.clone.1 | loop fusion | flops 6291456 | bytes 4194304 | tf_op jit(solution)/shard_map/while
  657.7 15.4 %fusion.121 = bf16[2,64,16,64]{1,3,2,0:T(8,128)(2,1)} fusion(bf16[2,256,16,64]{1,3,2,0:T(8,128)(2,1)S(1)} %copy-done, f32[2,16,64,256]{3,2,1,0:T(8,128)} %fusion.119, f32[2,16,64,256]{3,2,1,0:T(8,128)} %get-tuple-element.600, f32[2,16,64]{2,1,0:T(8,128)S(1)} %get-tuple-element.601), kind=kOutput, calls=%fused_computation.23.clone.1 | convolution fusion | flops 70912256 | bytes 5513216 | tf_op jit(solution)/shard_map/while/body/eval_jaxpr/chqk,ckhd->cqhd/dot_general | solution.py:66
  675.0 4.8 broadcast_select_fusion.5
  685.8 16.0 %convolution_bitcast_fusion.7 = f32[2,256,16,64]{1,3,2,0:T(8,128)} fusion(bf16[2,64,16,64]{1,3,2,0:T(8,128)(2,1)S(1)} %copy-done.4, f32[2,16,64,256]{3,2,1,0:T(8,128)} %fusion.119, f32[2,16,64,256]{3,2,1,0:T(8,128)} %get-tuple-element.600, f32[2,16,64]{2,1,0:T(8,128)S(1)} %get-tuple-element.601), kind=kOutput, calls=%fused_computation.18.clone.1 | convolution fusion | flops 70781184 | bytes 6561792 | tf_op jit(solution)/shard_map/while/body/eval_jaxpr/chqk,cqhd->ckhd/dot_general | solution.py:68
  710.3 4.9 copy.97
  715.2 5.2 reshape.306
  723.0 4.1 select_dynamic-update-slice_fusion.6
  736.0 4.1 gather_fusion
  742.7 18.9 %pad_maximum_fusion.4 = bf16[4,262144]{1,0:T(4,128)(2,1)} fusion(bf16[4,87296]{1,0:T(4,128)(2,1)S(1)} %copy-done.2, bf16[4,87424]{1,0:T(4,128)(2,1)S(1)} %gather_fusion.1, bf16[4,87424]{1,0:T(4,128)(2,1)S(1)} %gather_fusion.2), kind=kLoop, calls=%fused_computation.10.clone.1 | loop fusion | flops 6291456 | bytes 4194304 | tf_op jit(solution)/shard_map/while
  799.9 15.4 %fusion.121 = bf16[2,64,16,64]{1,3,2,0:T(8,128)(2,1)} fusion(bf16[2,256,16,64]{1,3,2,0:T(8,128)(2,1)S(1)} %copy-done, f32[2,16,64,256]{3,2,1,0:T(8,128)} %fusion.119, f32[2,16,64,256]{3,2,1,0:T(8,128)} %get-tuple-element.600, f32[2,16,64]{2,1,0:T(8,128)S(1)} %get-tuple-element.601), kind=kOutput, calls=%fused_computation.23.clone.1 | convolution fusion | flops 70912256 | bytes 5513216 | tf_op jit(solution)/shard_map/while/body/eval_jaxpr/chqk,ckhd->cqhd/dot_general | solution.py:66
  817.2 4.8 broadcast_select_fusion.5
  828.1 16.0 %convolution_bitcast_fusion.7 = f32[2,256,16,64]{1,3,2,0:T(8,128)} fusion(bf16[2,64,16,64]{1,3,2,0:T(8,128)(2,1)S(1)} %copy-done.4, f32[2,16,64,256]{3,2,1,0:T(8,128)} %fusion.119, f32[2,16,64,256]{3,2,1,0:T(8,128)} %get-tuple-element.600, f32[2,16,64]{2,1,0:T(8,128)S(1)} %get-tuple-element.601), kind=kOutput, calls=%fused_computation.18.clone.1 | convolution fusion | flops 70781184 | bytes 6561792 | tf_op jit(solution)/shard_map/while/body/eval_jaxpr/chqk,cqhd->ckhd/dot_general | solution.py:68
  852.6 4.9 copy.97
  857.5 5.2 reshape.306
  885.1 18.7 %pad_maximum_fusion.4 = bf16[4,262144]{1,0:T(4,128)(2,1)} fusion(bf16[4,87296]{1,0:T(4,128)(2,1)S(1)} %copy-done.2, bf16[4,87424]{1,0:T(4,128)(2,1)S(1)} %gather_fusion.1, bf16[4,87424]{1,0:T(4,128)(2,1)S(1)} %gather_fusion.2), kind=kLoop, calls=%fused_computation.10.clone.1 | loop fusion | flops 6291456 | bytes 4194304 | tf_op jit(solution)/shard_map/while
  942.1 15.4 %fusion.121 = bf16[2,64,16,64]{1,3,2,0:T(8,128)(2,1)} fusion(bf16[2,256,16,64]{1,3,2,0:T(8,128)(2,1)S(1)} %copy-done, f32[2,16,64,256]{3,2,1,0:T(8,128)} %fusion.119, f32[2,16,64,256]{3,2,1,0:T(8,128)} %get-tuple-element.600, f32[2,16,64]{2,1,0:T(8,128)S(1)} %get-tuple-element.601), kind=kOutput, calls=%fused_computation.23.clone.1 | convolution fusion | flops 70912256 | bytes 5513216 | tf_op jit(solution)/shard_map/while/body/eval_jaxpr/chqk,ckhd->cqhd/dot_general | solution.py:66
  959.4 4.8 broadcast_select_fusion.5
  970.5 16.0 %convolution_bitcast_fusion.7 = f32[2,256,16,64]{1,3,2,0:T(8,128)} fusion(bf16[2,64,16,64]{1,3,2,0:T(8,128)(2,1)S(1)} %copy-done.4, f32[2,16,64,256]{3,2,1,0:T(8,128)} %fusion.119, f32[2,16,64,256]{3,2,1,0:T(8,128)} %get-tuple-element.600, f32[2,16,64]{2,1,0:T(8,128)S(1)} %get-tuple-element.601), kind=kOutput, calls=%fused_computation.18.clone.1 | convolution fusion | flops 70781184 | bytes 6561792 | tf_op jit(solution)/shard_map/while/body/eval_jaxpr/chqk,cqhd->ckhd/dot_general | solution.py:68
  995.0 4.9 copy.97
  999.9 5.2 reshape.306
  1027.2 18.7 %pad_maximum_fusion.4 = bf16[4,262144]{1,0:T(4,128)(2,1)} fusion(bf16[4,87296]{1,0:T(4,128)(2,1)S(1)} %copy-done.2, bf16[4,87424]{1,0:T(4,128)(2,1)S(1)} %gather_fusion.1, bf16[4,87424]{1,0:T(4,128)(2,1)S(1)} %gather_fusion.2), kind=kLoop, calls=%fused_computation.10.clone.1 | loop fusion | flops 6291456 | bytes 4194304 | tf_op jit(solution)/shard_map/while
  1084.5 15.4 %fusion.121 = bf16[2,64,16,64]{1,3,2,0:T(8,128)(2,1)} fusion(bf16[2,256,16,64]{1,3,2,0:T(8,128)(2,1)S(1)} %copy-done, f32[2,16,64,256]{3,2,1,0:T(8,128)} %fusion.119, f32[2,16,64,256]{3,2,1,0:T(8,128)} %get-tuple-element.600, f32[2,16,64]{2,1,0:T(8,128)S(1)} %get-tuple-element.601), kind=kOutput, calls=%fused_computation.23.clone.1 | convolution fusion | flops 70912256 | bytes 5513216 | tf_op jit(solution)/shard_map/while/body/eval_jaxpr/chqk,ckhd->cqhd/dot_general | solution.py:66
  1101.8 4.8 broadcast_select_fusion.5
  1112.6 16.0 %convolution_bitcast_fusion.7 = f32[2,256,16,64]{1,3,2,0:T(8,128)} fusion(bf16[2,64,16,64]{1,3,2,0:T(8,128)(2,1)S(1)} %copy-done.4, f32[2,16,64,256]{3,2,1,0:T(8,128)} %fusion.119, f32[2,16,64,256]{3,2,1,0:T(8,128)} %get-tuple-element.600, f32[2,16,64]{2,1,0:T(8,128)S(1)} %get-tuple-element.601), kind=kOutput, calls=%fused_computation.18.clone.1 | convolution fusion | flops 70781184 | bytes 6561792 | tf_op jit(solution)/shard_map/while/body/eval_jaxpr/chqk,cqhd->ckhd/dot_general | solution.py:68
  1137.1 4.9 copy.97
  1142.0 5.2 reshape.306
  1166.0 4.5 convolution_bitcast_fusion.2
  1172.9 4.8 fusion.36
  1178.6 19.3 %reshape.244 = f32[16,262144]{1,0:T(8,128)} reshape(f32[4,4,262144]{2,1,0:T(4,128)} %get-tuple-element.365) | data formatting | bytes 33554432 | tf_op jit(solution)/shard_map/reshape | solution.py:172
  1197.9 11.1 fusion.35
  1209.5 6.6 reduce.4
  1216.1 8.3 reshape.277
  1224.3 6.3 all-to-all-start
  1232.0 112.1 %all-to-all-done = bf16[8,2,131072]{2,1,0:T(2,128)(2,1)} async-done(((bf16[8,2,131072]{2,1,0:T(2,128)(2,1)}), bf16[8,2,131072]{2,1,0:T(2,128)(2,1)}, u32[]{:S(2)}, u32[]{:S(2)}) %all-to-all-start) | async-done | bytes 4194336 | tf_op jit(solution)/shard_map/all_to_all | solution.py:192
  1344.1 8.8 reshape.278
  1352.9 9.1 convolution_convert_fusion.5
  1363.2 29.9 %reduce-scatter.2.cloned.1.call-done = bf16[256,2048]{0,1:T(8,128)(2,1)} async-done(((bf16[2048,2048]{0,1:T(8,128)(2,1)}), bf16[256,2048]{0,1:T(8,128)(2,1)}) %reduce-scatter.2.cloned.1.call-update) | async-done | bytes 1048592 | tf_op jit(solution)/shard_map/reduce_scatter | solution.py:184
  (415 shorter events, 532.6 us)
Async XLA Ops:
  7.2 3.1 copy-start.9
  7.2 3.2 copy-start.12
  7.2 3.4 copy-start.11
  7.2 127.4 %all-gather.3.cloned.1.call-start = ((), (), s32[]{:S(2)}) async-start(), calls=%async_computation.3 | async-start | bytes 9437184 | tf_op jit(solution)/shard_map/all_gather | solution.py:117
  10.2 1382.9 %reduce-scatter.2.cloned.1.call-start = ((), (), s32[]{:S(2)}) async-start(), calls=%async_computation.2 | async-start | bytes 9437184 | tf_op jit(solution)/shard_map/reduce_scatter | solution.py:184
  171.0 1.2 copy-start.2
  221.3 3.5 copy-start.1
  222.5 4.2 copy-start
  247.0 8.0 copy-start.3
  251.8 52.4 %collective-permute-start = (bf16[128,2048]{1,0:T(8,128)(2,1)}, bf16[128,2048]{1,0:T(8,128)(2,1)}, u32[]{:S(2)}, u32[]{:S(2)}) collective-permute-start(bf16[128,2048]{1,0:T(8,128)(2,1)} %get-tuple-element.602), channel_id=1, source_target_pairs={{8,0},{16,8},{24,16},{9,1},{17,9},{25,17},{10,2},{18,10},{26,18},{... | collective-permute-start | bytes 1572872 | tf_op jit(solution)/shard_map/while/body/eval_jaxpr/ppermute | solution.py:19
  256.7 2.2 copy-start.4
  258.9 16.1 %copy-start.6 = (bf16[2,64,16,64]{1,3,2,0:T(8,128)(2,1)S(1)}, bf16[2,64,16,64]{1,3,2,0:T(8,128)(2,1)}, u32[]{:S(2)}) copy-start(bf16[2,64,16,64]{1,3,2,0:T(8,128)(2,1)} %fusion.122) | copy-start | bytes 786436 | tf_op jit(solution)/shard_map/while
  300.1 3.2 copy-start.5
  314.5 1.2 copy-start.2
  364.6 3.5 copy-start.1
  365.7 4.2 copy-start
  390.3 7.0 copy-start.3
  395.1 51.4 %collective-permute-start = (bf16[128,2048]{1,0:T(8,128)(2,1)}, bf16[128,2048]{1,0:T(8,128)(2,1)}, u32[]{:S(2)}, u32[]{:S(2)}) collective-permute-start(bf16[128,2048]{1,0:T(8,128)(2,1)} %get-tuple-element.602), channel_id=1, source_target_pairs={{8,0},{16,8},{24,16},{9,1},{17,9},{25,17},{10,2},{18,10},{26,18},{... | collective-permute-start | bytes 1572872 | tf_op jit(solution)/shard_map/while/body/eval_jaxpr/ppermute | solution.py:19
  399.0 2.2 copy-start.4
  401.1 16.1 %copy-start.6 = (bf16[2,64,16,64]{1,3,2,0:T(8,128)(2,1)S(1)}, bf16[2,64,16,64]{1,3,2,0:T(8,128)(2,1)}, u32[]{:S(2)}) copy-start(bf16[2,64,16,64]{1,3,2,0:T(8,128)(2,1)} %fusion.122) | copy-start | bytes 786436 | tf_op jit(solution)/shard_map/while
  442.4 3.2 copy-start.5
  456.9 1.2 copy-start.2
  506.8 3.5 copy-start.1
  508.0 4.2 copy-start
  532.5 7.2 copy-start.3
  537.4 51.6 %collective-permute-start = (bf16[128,2048]{1,0:T(8,128)(2,1)}, bf16[128,2048]{1,0:T(8,128)(2,1)}, u32[]{:S(2)}, u32[]{:S(2)}) collective-permute-start(bf16[128,2048]{1,0:T(8,128)(2,1)} %get-tuple-element.602), channel_id=1, source_target_pairs={{8,0},{16,8},{24,16},{9,1},{17,9},{25,17},{10,2},{18,10},{26,18},{... | collective-permute-start | bytes 1572872 | tf_op jit(solution)/shard_map/while/body/eval_jaxpr/ppermute | solution.py:19
  541.4 2.2 copy-start.4
  543.6 16.1 %copy-start.6 = (bf16[2,64,16,64]{1,3,2,0:T(8,128)(2,1)S(1)}, bf16[2,64,16,64]{1,3,2,0:T(8,128)(2,1)}, u32[]{:S(2)}) copy-start(bf16[2,64,16,64]{1,3,2,0:T(8,128)(2,1)} %fusion.122) | copy-start | bytes 786436 | tf_op jit(solution)/shard_map/while
  584.8 3.2 copy-start.5
  599.1 1.2 copy-start.2
  649.3 3.5 copy-start.1
  650.4 4.2 copy-start
  675.0 6.9 copy-start.3
  679.8 51.4 %collective-permute-start = (bf16[128,2048]{1,0:T(8,128)(2,1)}, bf16[128,2048]{1,0:T(8,128)(2,1)}, u32[]{:S(2)}, u32[]{:S(2)}) collective-permute-start(bf16[128,2048]{1,0:T(8,128)(2,1)} %get-tuple-element.602), channel_id=1, source_target_pairs={{8,0},{16,8},{24,16},{9,1},{17,9},{25,17},{10,2},{18,10},{26,18},{... | collective-permute-start | bytes 1572872 | tf_op jit(solution)/shard_map/while/body/eval_jaxpr/ppermute | solution.py:19
  683.6 2.2 copy-start.4
  685.8 16.1 %copy-start.6 = (bf16[2,64,16,64]{1,3,2,0:T(8,128)(2,1)S(1)}, bf16[2,64,16,64]{1,3,2,0:T(8,128)(2,1)}, u32[]{:S(2)}) copy-start(bf16[2,64,16,64]{1,3,2,0:T(8,128)(2,1)} %fusion.122) | copy-start | bytes 786436 | tf_op jit(solution)/shard_map/while
  727.1 3.2 copy-start.5
  741.4 1.2 copy-start.2
  791.5 3.5 copy-start.1
  792.6 4.2 copy-start
  817.2 7.0 copy-start.3
  822.0 51.4 %collective-permute-start = (bf16[128,2048]{1,0:T(8,128)(2,1)}, bf16[128,2048]{1,0:T(8,128)(2,1)}, u32[]{:S(2)}, u32[]{:S(2)}) collective-permute-start(bf16[128,2048]{1,0:T(8,128)(2,1)} %get-tuple-element.602), channel_id=1, source_target_pairs={{8,0},{16,8},{24,16},{9,1},{17,9},{25,17},{10,2},{18,10},{26,18},{... | collective-permute-start | bytes 1572872 | tf_op jit(solution)/shard_map/while/body/eval_jaxpr/ppermute | solution.py:19
  825.9 2.2 copy-start.4
  828.0 16.1 %copy-start.6 = (bf16[2,64,16,64]{1,3,2,0:T(8,128)(2,1)S(1)}, bf16[2,64,16,64]{1,3,2,0:T(8,128)(2,1)}, u32[]{:S(2)}) copy-start(bf16[2,64,16,64]{1,3,2,0:T(8,128)(2,1)} %fusion.122) | copy-start | bytes 786436 | tf_op jit(solution)/shard_map/while
  869.3 3.2 copy-start.5
  883.8 1.2 copy-start.2
  933.7 3.5 copy-start.1
  934.9 4.2 copy-start
  959.4 7.2 copy-start.3
  964.2 51.6 %collective-permute-start = (bf16[128,2048]{1,0:T(8,128)(2,1)}, bf16[128,2048]{1,0:T(8,128)(2,1)}, u32[]{:S(2)}, u32[]{:S(2)}) collective-permute-start(bf16[128,2048]{1,0:T(8,128)(2,1)} %get-tuple-element.602), channel_id=1, source_target_pairs={{8,0},{16,8},{24,16},{9,1},{17,9},{25,17},{10,2},{18,10},{26,18},{... | collective-permute-start | bytes 1572872 | tf_op jit(solution)/shard_map/while/body/eval_jaxpr/ppermute | solution.py:19
  968.3 2.2 copy-start.4
  970.5 16.1 %copy-start.6 = (bf16[2,64,16,64]{1,3,2,0:T(8,128)(2,1)S(1)}, bf16[2,64,16,64]{1,3,2,0:T(8,128)(2,1)}, u32[]{:S(2)}) copy-start(bf16[2,64,16,64]{1,3,2,0:T(8,128)(2,1)} %fusion.122) | copy-start | bytes 786436 | tf_op jit(solution)/shard_map/while
  1011.7 3.2 copy-start.5
  1026.0 1.2 copy-start.2
  1076.1 3.5 copy-start.1
  1077.2 4.2 copy-start
  1101.8 6.9 copy-start.3
  1106.6 51.3 %collective-permute-start = (bf16[128,2048]{1,0:T(8,128)(2,1)}, bf16[128,2048]{1,0:T(8,128)(2,1)}, u32[]{:S(2)}, u32[]{:S(2)}) collective-permute-start(bf16[128,2048]{1,0:T(8,128)(2,1)} %get-tuple-element.602), channel_id=1, source_target_pairs={{8,0},{16,8},{24,16},{9,1},{17,9},{25,17},{10,2},{18,10},{26,18},{... | collective-permute-start | bytes 1572872 | tf_op jit(solution)/shard_map/while/body/eval_jaxpr/ppermute | solution.py:19
  1110.4 2.2 copy-start.4
  1112.6 16.1 %copy-start.6 = (bf16[2,64,16,64]{1,3,2,0:T(8,128)(2,1)S(1)}, bf16[2,64,16,64]{1,3,2,0:T(8,128)(2,1)}, u32[]{:S(2)}) copy-start(bf16[2,64,16,64]{1,3,2,0:T(8,128)(2,1)} %fusion.122) | copy-start | bytes 786436 | tf_op jit(solution)/shard_map/while
  1153.9 3.2 copy-start.5
  1165.9 4.5 copy-start.7
  1166.0 4.5 copy-start.8
  1224.3 119.8 %all-to-all-start = ((bf16[8,2,131072]{2,1,0:T(2,128)(2,1)}), bf16[8,2,131072]{2,1,0:T(2,128)(2,1)}, u32[]{:S(2)}, u32[]{:S(2)}) async-start(bf16[8,2,131072]{2,1,0:T(2,128)(2,1)} %reshape.277), calls=%async_computation.1 | async-start | bytes 8388608 | tf_op jit(solution)/shard_map/all_to_all | solution.py:192
  (1 other events, 0.7 us)
Sparse Core Ops, SparseCore 0:
  10.7 123.8 all-gather.2
  1177.9 215.2 reduce-scatter.1
where the time goes:
time: 1420 us; the launch traced here: 1400 us
  local copies, waits for them, and re-layouts  454 us (32%)
  matrix products  389 us (27%)
  waiting for transfers between devices  266 us (19%)
  other arithmetic  247 us (17%)
  starting transfers between devices  22.6 us (2%)
  between operations  14.7 us (1%)
    while x7, other arithmetic  131 us
    all_gather x1, waiting for transfers between devices, body(): whole_pool = lax.all_gather(owned_flat, 'dp', axis=0, tiled=True)  124 us
    dot_general x7, matrix products, section_backward(): jnp.einsum('chqk,cqhd->ckhd', d_scores, heads_q, preferred_element_type=j...  112 us
    all_to_all x1, waiting for transfers between devices, body(): lax.all_to_all(partial_sum.astype(jnp.bfloat16), 'dp', split_axis=0, conc...  112 us
    dot_general x7, matrix products, section_backward(): jnp.einsum('chqk,ckhd->cqhd', d_scores, key_rows, preferred_element_type=...  108 us
    gather x42, local copies, waits for them, and re-layouts, section_backward(): blocks = jnp.take(fetched, ref_owner, axis=0)  103 us
    dynamic_update_slice x28, other arithmetic, place_row(): lax.dynamic_update_index_in_dim(store, jnp.where(is_valid, value, previou...  66 us
    reshape x14, local copies, waits for them, and re-layouts, section_backward(): jnp.stack([d_keys.reshape(spans * K_NBR, NBR_LEN * inner_width), d_values...  63.2 us
  transfers between devices with their start and end apart: 10, of which 3 were waited for; matrix products, arithmetic and copies ran while one was open for 29% of the time, Pallas kernels for 0%

commit v1 on v0

v1 whole, which is shorter than its diff:
```python
import functools

import jax
import jax.numpy as jnp
from jax import lax
from jax.experimental import pallas as pl
from jax.experimental.pallas import tpu as pltpu
from jax.sharding import PartitionSpec as P

HEADS = 16
HEAD_DIM = 64
SPAN = 64
K_NBR = 2
NBR_LEN = 128
PAIR = 2 * HEAD_DIM
KEYS = K_NBR * NBR_LEN
SCALE = HEAD_DIM ** (-0.5)
BF = jnp.bfloat16
F32 = jnp.float32
ANY = pl.BlockSpec(memory_space=pl.ANY)


def nt(a, b):
    return lax.dot_general(a, b, (((1,), (1,)), ((), ())), preferred_element_type=F32)


def nn(a, b):
    return lax.dot_general(a, b, (((1,), (0,)), ((), ())), preferred_element_type=F32)


def tn(a, b):
    return lax.dot_general(a, b, (((0,), (0,)), ((), ())), preferred_element_type=F32)


def head_rows(x):
    heads = x.shape[1] // HEAD_DIM
    if heads == 1:
        return x
    lane = lax.broadcasted_iota(jnp.int32, x.shape, 1) // HEAD_DIM
    zero = jnp.zeros_like(x)
    return jnp.concatenate([jnp.where(lane == h, x, zero) for h in range(heads)], axis=0)


def head_columns(y):
    heads = y.shape[1] // HEAD_DIM
    out = y[:SPAN]
    lane = lax.broadcasted_iota(jnp.int32, out.shape, 1) // HEAD_DIM
    for h in range(1, heads):
        out = jnp.where(lane == h, y[h * SPAN : (h + 1) * SPAN], out)
    return out


def softmax_rows(scores):
    weights = jnp.exp(scores - jnp.max(scores, axis=-1, keepdims=True))
    return weights / jnp.sum(weights, axis=-1, keepdims=True)


def probs_kernel(owners, q_ref, k_ref, out_ref):
    micro = pl.program_id(0)
    tokens, width = q_ref.shape[1], q_ref.shape[2]
    spans = tokens // SPAN
    for span in range(spans):
        refs = [owners[(micro * spans + span) * K_NBR + k] for k in range(K_NBR)]
        for pair in range(width // PAIR):
            cols = slice(pair * PAIR, (pair + 1) * PAIR)
            keys = jnp.concatenate([k_ref[r, :, cols] for r in refs], axis=0)
            rows = head_rows(q_ref[0, span * SPAN : (span + 1) * SPAN, cols])
            out_ref[0, span * (width // PAIR) + pair] = softmax_rows(nt(rows, keys) * SCALE).astype(BF)


def tick_kernel(
    chunks,
    scal,
    arriving, top, w_out, w_query, keys, values, probs, g0, q0, a0, u0, d0,
    leaving, g_store, q_store, a_store, u_store, d_store,
    up, wo, wq, kb, vb, pb, datt, dq, att, gr, sem_up, sem_wo, sem_wq, sem_k, sem_v, sem_p, sem_out,
):
    micro = scal[0]
    valid = scal[1]
    last = scal[2]
    tokens = up.shape[0]
    spans = tokens // SPAN
    refs = spans * K_NBR
    pairs = datt.shape[1] // PAIR
    rows = w_out.shape[0] // chunks

    def copy_wo(c):
        return pltpu.make_async_copy(w_out.at[pl.ds(c * rows, rows)], wo.at[c], sem_wo.at[c])

    def copy_wq(c):
        return pltpu.make_async_copy(w_query.at[pl.ds(c * rows, rows)], wq.at[c], sem_wq.at[c])

    def copy_v(i):
        return pltpu.make_async_copy(values.at[scal[3 + i]], vb.at[i], sem_v.at[i])

    def copy_k(i):
        return pltpu.make_async_copy(keys.at[scal[3 + i]], kb.at[i], sem_k.at[i])

    @pl.when(valid > 0)
    def _():
        from_top = pltpu.make_async_copy(top.at[micro], up, sem_up)
        from_hop = pltpu.make_async_copy(arriving, up, sem_up)

        @pl.when(last > 0)
        def _():
            from_top.start()

        @pl.when(last == 0)
        def _():
            from_hop.start()

        for c in range(chunks):
            copy_wo(c).start()
        for i in range(refs):
            copy_v(i).start()
        get_probs = pltpu.make_async_copy(probs.at[micro], pb, sem_p)
        get_probs.start()
        for i in range(refs):
            copy_k(i).start()
        for c in range(chunks):
            copy_wq(c).start()
        from_hop.wait()
        save_up = pltpu.make_async_copy(up, u_store.at[micro], sem_out.at[0])
        save_up.start()
        acc = None
        for c in range(chunks):
            copy_wo(c).wait()
            part = nn(up[:, c * rows : (c + 1) * rows], wo[c])
            acc = part if acc is None else acc + part
        datt[...] = acc.astype(BF)
        save_d = pltpu.make_async_copy(datt, d_store.at[micro], sem_out.at[1])
        save_d.start()
        for i in range(refs):
            copy_v(i).wait()
        get_probs.wait()
        for i in range(refs):
            copy_k(i).wait()
        for span in range(spans):
            rws = slice(span * SPAN, (span + 1) * SPAN)
            for pair in range(pairs):
                cols = slice(pair * PAIR, (pair + 1) * PAIR)
                val = jnp.concatenate([vb[span * K_NBR + k, :, cols] for k in range(K_NBR)], axis=0)
                key = jnp.concatenate([kb[span * K_NBR + k, :, cols] for k in range(K_NBR)], axis=0)
                prob_b = pb[span * pairs + pair]
                d_probs = nt(head_rows(datt[rws, cols]), val)
                prob = prob_b.astype(F32)
                delta = jnp.sum(prob * d_probs, axis=-1, keepdims=True)
                d_scores = (prob * (d_probs - delta) * SCALE).astype(BF)
                dq[rws, cols] = head_columns(nn(d_scores, key)).astype(BF)
                att[rws, cols] = head_columns(nn(prob_b, val)).astype(BF)
        save_q = pltpu.make_async_copy(dq, q_store.at[micro], sem_out.at[2])
        save_q.start()
        save_a = pltpu.make_async_copy(att, a_store.at[micro], sem_out.at[3])
        save_a.start()
        for c in range(chunks):
            copy_wq(c).wait()
            cols = slice(c * rows, (c + 1) * rows)
            gr[:, cols] = (up[:, cols].astype(F32) + nt(dq[...], wq[c])).astype(BF)
        send = pltpu.make_async_copy(gr, leaving, sem_out.at[4])
        send.start()
        save_g = pltpu.make_async_copy(gr, g_store.at[micro], sem_out.at[5])
        save_g.start()
        for c in (save_up, save_d, save_q, save_a, send, save_g):
            c.wait()


def block_grads_kernel(ids, mask, q_ref, d_ref, kv_ref, out_ref, acc):
    reader = pl.program_id(0)
    micros, tokens, width = q_ref.shape[1], q_ref.shape[2], q_ref.shape[3]
    spans = tokens // SPAN
    readers = pl.num_programs(0)

    @pl.when(reader == 0)
    def _():
        acc[...] = jnp.zeros_like(acc)

    for micro in range(micros):
        for span in range(spans):
            at = [((micro * readers + reader) * spans + span) * K_NBR + k for k in range(K_NBR)]
            rws = slice(span * SPAN, (span + 1) * SPAN)
            refs = [ids[i] for i in at]
            keep = [mask[i] > 0 for i in at]
            zero = jnp.zeros((NBR_LEN, width), BF)
            key = jnp.concatenate([jnp.where(m, kv_ref[r, 0], zero) for m, r in zip(keep, refs)], axis=0)
            val = jnp.concatenate([jnp.where(m, kv_ref[r, 1], zero) for m, r in zip(keep, refs)], axis=0)
            q_rows = head_rows(q_ref[0, micro, rws])
            d_rows = head_rows(d_ref[0, micro, rws])
            prob = softmax_rows(nt(q_rows, key) * SCALE)
            d_probs = nt(d_rows, val)
            delta = jnp.sum(prob * d_probs, axis=-1, keepdims=True)
            d_scores = (prob * (d_probs - delta) * SCALE).astype(BF)
            d_keys = tn(d_scores, q_rows)
            d_values = tn(prob.astype(BF), d_rows)
            fzero = jnp.zeros((NBR_LEN, width), F32)
            for k in range(K_NBR):
                part = slice(k * NBR_LEN, (k + 1) * NBR_LEN)
                acc[refs[k], 0] += jnp.where(keep[k], d_keys[part], fzero)
                acc[refs[k], 1] += jnp.where(keep[k], d_values[part], fzero)

    @pl.when(reader == readers - 1)
    def _():
        out_ref[...] = acc[...].astype(BF)


def body(
    section_inputs,
    top_grads,
    query_weight,
    output_weight,
    neighbour_kv,
    nbr_ids,
    send_list,
    send_counts,
):
    n_section = lax.axis_size("section")
    section_index = lax.axis_index("section")
    n_data = lax.axis_size("dp")
    data_index = lax.axis_index("dp")
    inputs_all = section_inputs[0]
    w_query = query_weight[0]
    w_out = output_weight[0]
    owned = neighbour_kv[0]
    micros, tokens, model = inputs_all.shape
    blk_dev = owned.shape[0]
    width = w_query.shape[1]
    spans = tokens // SPAN
    slice_w = width // n_data
    params = functools.partial(pltpu.CompilerParams, vmem_limit_bytes=56 << 20)

    my_list = lax.dynamic_index_in_dim(send_list, data_index, 0, keepdims=False)
    my_counts = lax.dynamic_index_in_dim(send_counts, data_index, 0, keepdims=False)

    def outbound(which):
        picked = jnp.zeros((n_data, NBR_LEN, width), BF)
        for b in range(blk_dev):
            chosen = ((my_list == b) & (my_counts > 0))[:, None, None]
            picked = jnp.where(chosen, owned[b, which][None], picked)
        return picked

    def exchange(x):
        return lax.all_to_all(x, "dp", split_axis=0, concat_axis=0, tiled=True)

    keys = exchange(outbound(0))
    values = exchange(outbound(1))
    query = nn(inputs_all.reshape(micros * tokens, model), w_query).astype(BF)
    query = query.reshape(micros, tokens, width)
    owners = (nbr_ids // blk_dev).astype(jnp.int32)

    probs = pl.pallas_call(
        probs_kernel,
        out_shape=jax.ShapeDtypeStruct((micros, spans * width // PAIR, 2 * SPAN, KEYS), BF),
        grid_spec=pltpu.PrefetchScalarGridSpec(
            num_scalar_prefetch=1,
            grid=(micros,),
            in_specs=[
                pl.BlockSpec((1, tokens, width), lambda i, o: (i, 0, 0)),
                pl.BlockSpec((n_data, NBR_LEN, width), lambda i, o: (0, 0, 0)),
            ],
            out_specs=pl.BlockSpec((1, spans * width // PAIR, 2 * SPAN, KEYS), lambda i, o: (i, 0, 0, 0)),
        ),
        compiler_params=params(),
    )(owners.reshape(-1), query, keys)

    chunks = 4
    lag = 2 * (n_section - 1 - section_index)
    last = (section_index == n_section - 1).astype(jnp.int32)
    refs = spans * K_NBR
    tick = pl.pallas_call(
        functools.partial(tick_kernel, chunks),
        out_shape=(
            jax.ShapeDtypeStruct((tokens, model), BF),
            jax.ShapeDtypeStruct((micros, tokens, model), BF),
            jax.ShapeDtypeStruct((micros, tokens, width), BF),
            jax.ShapeDtypeStruct((micros, tokens, width), BF),
            jax.ShapeDtypeStruct((micros, tokens, model), BF),
            jax.ShapeDtypeStruct((micros, tokens, width), BF),
        ),
        grid_spec=pltpu.PrefetchScalarGridSpec(
            num_scalar_prefetch=1,
            grid=(1,),
            in_specs=[ANY] * 12,
            out_specs=[ANY] * 6,
            scratch_shapes=[
                pltpu.VMEM((tokens, model), BF),
                pltpu.VMEM((chunks, model // chunks, width), BF),
                pltpu.VMEM((chunks, model // chunks, width), BF),
                pltpu.VMEM((refs, NBR_LEN, width), BF),
                pltpu.VMEM((refs, NBR_LEN, width), BF),
                pltpu.VMEM((spans * width // PAIR, 2 * SPAN, KEYS), BF),
                pltpu.VMEM((tokens, width), BF),
                pltpu.VMEM((tokens, width), BF),
                pltpu.VMEM((tokens, width), BF),
                pltpu.VMEM((tokens, model), BF),
                pltpu.SemaphoreType.DMA,
                pltpu.SemaphoreType.DMA((chunks,)),
                pltpu.SemaphoreType.DMA((chunks,)),
                pltpu.SemaphoreType.DMA((refs,)),
                pltpu.SemaphoreType.DMA((refs,)),
                pltpu.SemaphoreType.DMA,
                pltpu.SemaphoreType.DMA((6,)),
            ],
        ),
        input_output_aliases={8: 1, 9: 2, 10: 3, 11: 4, 12: 5},
        compiler_params=params(),
    )
    hop_pairs = [(i, i - 1) for i in range(1, n_section)]

    def run_tick(index, state):
        arriving, leaving, stores = state
        coming = lax.ppermute(leaving, "section", hop_pairs)
        micro_now = index - lag
        valid = ((micro_now >= 0) & (micro_now < micros)).astype(jnp.int32)
        slot = jnp.clip(micro_now, 0, micros - 1)
        mine = lax.dynamic_index_in_dim(owners, slot, 0, keepdims=False).reshape(-1)
        scal = jnp.concatenate([jnp.stack([slot, valid, last]).astype(jnp.int32), mine])
        out = tick(scal, arriving, top_grads, w_out, w_query, keys, values, probs, *stores)
        return coming, out[0], out[1:]

    stores = (
        jnp.zeros((micros, tokens, model), BF),
        jnp.zeros((micros, tokens, width), BF),
        jnp.zeros((micros, tokens, width), BF),
        jnp.zeros((micros, tokens, model), BF),
        jnp.zeros((micros, tokens, width), BF),
    )
    empty = jnp.zeros((tokens, model), BF)
    ticks = micros + 2 * (n_section - 1)
    _, _, stores = lax.fori_loop(0, ticks, run_tick, (empty, empty, stores))
    grads_in, d_query, attended, upstream, d_attended = stores

    flat = micros * tokens
    grad_scale = (flat * n_data) ** (-0.5)
    query_term = tn(inputs_all.reshape(flat, model), d_query.reshape(flat, width))
    output_term = tn(upstream.reshape(flat, model), attended.reshape(flat, width))
    shares = lax.psum_scatter(
        (jnp.concatenate([query_term, output_term], axis=1) * grad_scale).astype(BF),
        "dp",
        scatter_dimension=0,
        tiled=True,
    )

    def by_heads(x):
        lead = x.shape[:-1]
        x = jnp.moveaxis(x.reshape(*lead, n_data, slice_w), -2, 0)
        return exchange(x)

    kv_heads = by_heads(owned).reshape(n_data * blk_dev, 2, NBR_LEN, slice_w)
    q_heads = by_heads(query)
    d_heads = by_heads(d_attended)
    ids_all = lax.all_gather(nbr_ids, "dp", axis=1, tiled=True)
    owner_all = ids_all // blk_dev
    reader_all = (jnp.arange(n_data * spans, dtype=jnp.int32) // spans)[None, :, None]
    hit_owner = owner_all[..., None] == jnp.arange(n_data, dtype=jnp.int32)
    list_r = jnp.take(send_list, reader_all[0, :, 0], axis=1).T[None, :, None, :]
    count_r = jnp.take(send_counts, reader_all[0, :, 0], axis=1).T[None, :, None, :]
    block_all = owner_all * blk_dev + jnp.sum(jnp.where(hit_owner, list_r, 0), axis=-1)
    mask_all = jnp.sum(jnp.where(hit_owner, count_r, 0), axis=-1)
    blocks = n_data * blk_dev
    block_grads = pl.pallas_call(
        block_grads_kernel,
        out_shape=jax.ShapeDtypeStruct((blocks, 2, NBR_LEN, slice_w), BF),
        grid_spec=pltpu.PrefetchScalarGridSpec(
            num_scalar_prefetch=2,
            grid=(n_data,),
            in_specs=[
                pl.BlockSpec((1, micros, tokens, slice_w), lambda i, a, b: (i, 0, 0, 0)),
                pl.BlockSpec((1, micros, tokens, slice_w), lambda i, a, b: (i, 0, 0, 0)),
                pl.BlockSpec((blocks, 2, NBR_LEN, slice_w), lambda i, a, b: (0, 0, 0, 0)),
            ],
            out_specs=pl.BlockSpec((blocks, 2, NBR_LEN, slice_w), lambda i, a, b: (0, 0, 0, 0)),
            scratch_shapes=[pltpu.VMEM((blocks, 2, NBR_LEN, slice_w), F32)],
        ),
        compiler_params=params(),
    )(block_all.reshape(-1).astype(jnp.int32), mask_all.reshape(-1).astype(jnp.int32), q_heads, d_heads, kv_heads)
    returned = exchange(block_grads.reshape(n_data, blk_dev, 2, NBR_LEN, slice_w))
    kv_grads = jnp.moveaxis(returned, 0, -2).reshape(blk_dev, 2, NBR_LEN, width)
    return (
        grads_in[None],
        shares[None, :, :width],
        shares[None, :, width:],
        kv_grads[None],
    )


def solution(mesh):
    in_specs = (
        P("section", None, "dp", None),
        P(None, "dp", None),
        P("section", None, None),
        P("section", None, None),
        P("section", "dp", None, None, None),
        P(None, "dp", None),
        P(),
        P(),
    )
    out_specs = (
        P("section", None, "dp", None),
        P("section", "dp", None),
        P("section", "dp", None),
        P("section", "dp", None, None, None),
    )
    return jax.shard_map(body, mesh=mesh, in_specs=in_specs, out_specs=out_specs, check_vma=False)
```

time: 1420 us -> 543 us (0.38)
  local copies, waits for them, and re-layouts: 454 us -> 66.7 us
  matrix products: 389 us -> 12 us
  other arithmetic: 247 us -> 13.6 us
  blocking collectives: 0 us -> 116 us
  waiting for transfers between devices: 266 us -> 163 us
  Pallas kernels: 0 us -> 96.9 us
  starting transfers between devices: 22.6 us -> 53.2 us
    dot_general x61 -> x3, matrix products: 367 us -> 12 us  [the longest x2 6.32 us: tn(): lax.dot_general(a, b, (((0,), (0,)), ((), ())), preferred_element_type=F32)]
    while x7 -> x0, other arithmetic: 131 us -> none
    reshape x64 -> x14, local copies, waits for them, and re-layouts: 132 us -> 5 us  [the longest x1 2.28 us: by_heads(): x = jnp.moveaxis(x.reshape(*lead, n_data, slice_w), -2, 0)]
    all_gather x1 -> x0, waiting for transfers between devices: 124 us -> none  [body(): whole_pool = lax.all_gather(owned_flat, 'dp', axis=0, tiled=True)]
    gather x42 -> x2, local copies, waits for them, and re-layouts: 103 us -> 1.12 us  [the longest x1 0.56 us: body(): jnp.take(send_counts, reader_all[0, :, 0], axis=1).T[None, :, None, :]]
    pallas_call x0 -> x12, Pallas kernels: none -> 96.9 us  [the longest x10 54.7 us: run_tick(): tick(scal, arriving, top_grads, w_out, w_query, keys, values, probs, *sto...]
    all_to_all x0 -> x2, blocking collectives: none -> 79.9 us  [exchange(): return lax.all_to_all(x, 'dp', split_axis=0, concat_axis=0, tiled=True)]
    dynamic_update_slice x28 -> x0, other arithmetic: 66 us -> none  [place_row(): lax.dynamic_update_index_in_dim(store, jnp.where(is_valid, value, previou...]
  transfers between devices with their start and end apart: 10 -> 15, of which waited for: 3 -> 9; matrix products, arithmetic and copies ran while one was open for 29% -> 5% of each run, Pallas kernels for 0% -> 18%
where the time goes in v1:
time: 543 us; the launch traced here: 537 us
  waiting for transfers between devices  163 us (30%)
  blocking collectives  116 us (21%)
  Pallas kernels  96.9 us (18%)
  local copies, waits for them, and re-layouts  66.7 us (12%)
  starting transfers between devices  53.2 us (10%)
  between operations  14.2 us (3%)
  other arithmetic  13.6 us (3%)
  matrix products  12 us (2%)
    all_to_all x4, waiting for transfers between devices, exchange(): return lax.all_to_all(x, 'dp', split_axis=0, concat_axis=0, tiled=True)  116 us
    all_to_all x2, blocking collectives, exchange(): return lax.all_to_all(x, 'dp', split_axis=0, concat_axis=0, tiled=True)  79.9 us
    pallas_call x10, Pallas kernels, run_tick(): tick(scal, arriving, top_grads, w_out, w_query, keys, values, probs, *sto...  54.7 us
    ppermute x10, waiting for transfers between devices, run_tick(): coming = lax.ppermute(leaving, 'section', hop_pairs)  47.1 us
    all_gather x1, blocking collectives, body(): ids_all = lax.all_gather(nbr_ids, 'dp', axis=1, tiled=True)  36.3 us
    pallas_call x1, Pallas kernels, body(): pl.pallas_call(block_grads_kernel, out_shape=jax.ShapeDtypeStruct((blocks...  35.5 us
    all_to_all x4, starting transfers between devices, exchange(): return lax.all_to_all(x, 'dp', split_axis=0, concat_axis=0, tiled=True)  33.6 us
    another operation x15, local copies, waits for them, and re-layouts  24.9 us
  transfers between devices with their start and end apart: 15, of which 9 were waited for; matrix products, arithmetic and copies ran while one was open for 5% of the time, Pallas kernels for 18%

profile of v1, /device:TPU:9, one launch (start us, length us, event | category | flops | bytes accessed | tf_op | source)
XLA Modules:
  0.0 536.6 jit_solution(12892916895049835969)
XLA Ops:
  7.2 1.4 slice_bitcast_fusion.3
  8.7 1.9 select_select_fusion
  10.6 52.0 %all_to_all.30.k_ref = bf16[8,128,1024]{2,1,0:T(8,128)(2,1)} all-to-all(bf16[8,128,1024]{2,1,0:T(8,128)(2,1)S(1)} %get-tuple-element.337), channel_id=1, replica_groups=mesh['section'=4,'dp'=8] {'dp'}, dimensions={0} | all-to-all | bytes 4194304 | tf_op jit(solution)/shard_map/all_to_all | solution.py:241
  62.6 5.4 %all-to-all-start.1 = ((bf16[8,128,1024]{2,1,0:T(8,128)(2,1)}), bf16[8,128,1024]{2,1,0:T(8,128)(2,1)}, u32[]{:S(2)}, u32[]{:S(2)}) async-start(bf16[8,128,1024]{2,1,0:T(8,128)(2,1)} %get-tuple-element.336), calls=%async_computation.1 | async-start | bytes 4194304 | tf_op jit(solution)/shard_map/all_to_all | solution.py:241
  68.7 5.6 %convolution_convert_fusion = bf16[512,1024]{1,0:T(8,128)(2,1)} fusion(bf16[512,2048]{1,0:T(8,128)(2,1)S(1)} %bitcast.70, bf16[1,2048,1024]{2,1,0:T(8,128)(2,1)} %param.14), kind=kOutput, calls=%fused_computation.10 | convolution fusion | flops 2148007936 | bytes 7340032 | tf_op jit(solution)/shard_map/dot_general | solution.py:28
  74.3 6.8 %shard_map.111 = bf16[4,16,128,256]{3,2,1,0:T(8,128)(2,1)} custom-call(s32[16]{0:T(128)} %reshape.82.owners, bf16[4,128,1024]{2,1,0:T(8,128)(2,1)} %bitcast.86, bf16[8,128,1024]{2,1,0:T(8,128)(2,1)S(1)} %copy-done.1), custom_call_target="tpu_custom_call" | custom-call | tf_op jit(solution)/shard_map/pallas_call | solution.py:249
  81.1 32.8 %all-to-all-done.1 = bf16[8,128,1024]{2,1,0:T(8,128)(2,1)} async-done(((bf16[8,128,1024]{2,1,0:T(8,128)(2,1)}), bf16[8,128,1024]{2,1,0:T(8,128)(2,1)}, u32[]{:S(2)}, u32[]{:S(2)}) %all-to-all-start.1) | async-done | bytes 2097184 | tf_op jit(solution)/shard_map/all_to_all | solution.py:241
  117.9 1.6 broadcast.86.clone
  119.6 1.6 broadcast.86
  121.2 167.5 %while.25 = (s32[]{:T(128)}, bf16[128,2048]{1,0:T(8,128)(2,1)}, bf16[128,2048]{1,0:T(8,128)(2,1)}, bf16[4,128,2048]{2,1,0:T(8,128)(2,1)}, bf16[4,128,1024]{2,1,0...) while((s32[]{:T(128)}, bf16[128,2048]{1,0:T(8,128)(2,1)}, ...), condition=%wide.region_1.2_spmd, body=%wide.region_0.1_spmd.sunk | while | flops 30 | bytes 4194719 | solution.py:328
  121.2 1.9 copy.106
  123.1 2.4 collective-permute-start
  127.2 6.7 %collective-permute-done = bf16[128,2048]{1,0:T(8,128)(2,1)} collective-permute-done((bf16[128,2048]{1,0:T(8,128)(2,1)}, bf16[128,2048]{1,0:T(8,128)(2,1)}, u32[]{:S(2)}, u32[]{:S(2)}) %collective-permute-start) | collective-permute-done | bytes 524320 | tf_op jit(solution)/shard_map/while/body/eval_jaxpr/ppermute | solution.py:310
  133.9 1.9 copy.113
  135.8 1.9 copy.106
  137.7 1.9 collective-permute-start
  141.3 7.2 %collective-permute-done = bf16[128,2048]{1,0:T(8,128)(2,1)} collective-permute-done((bf16[128,2048]{1,0:T(8,128)(2,1)}, bf16[128,2048]{1,0:T(8,128)(2,1)}, u32[]{:S(2)}, u32[]{:S(2)}) %collective-permute-start) | collective-permute-done | bytes 524320 | tf_op jit(solution)/shard_map/while/body/eval_jaxpr/ppermute | solution.py:310
  148.5 1.9 copy.113
  150.4 1.9 copy.106
  152.3 1.9 collective-permute-start
  155.9 7.2 %collective-permute-done = bf16[128,2048]{1,0:T(8,128)(2,1)} collective-permute-done((bf16[128,2048]{1,0:T(8,128)(2,1)}, bf16[128,2048]{1,0:T(8,128)(2,1)}, u32[]{:S(2)}, u32[]{:S(2)}) %collective-permute-start) | collective-permute-done | bytes 524320 | tf_op jit(solution)/shard_map/while/body/eval_jaxpr/ppermute | solution.py:310
  163.1 1.9 copy.113
  165.0 1.9 copy.106
  167.0 1.9 collective-permute-start
  170.5 11.5 %collective-permute-done = bf16[128,2048]{1,0:T(8,128)(2,1)} collective-permute-done((bf16[128,2048]{1,0:T(8,128)(2,1)}, bf16[128,2048]{1,0:T(8,128)(2,1)}, u32[]{:S(2)}, u32[]{:S(2)}) %collective-permute-start) | collective-permute-done | bytes 524320 | tf_op jit(solution)/shard_map/while/body/eval_jaxpr/ppermute | solution.py:310
  182.0 1.9 copy.113
  183.9 1.9 copy.106
  185.8 1.9 collective-permute-start
  188.5 12.3 %eval_jaxpr.5 = (bf16[128,2048]{1,0:T(8,128)(2,1)}, bf16[4,128,2048]{2,1,0:T(8,128)(2,1)}, bf16[4,128,1024]{2,1,0:T(8,128)(2,1)}, bf16[4,128,1024]{2,1,0:T(8,128...) custom-call(s32[7]{0:T(128)} %pad_add_fusion.2.scal, ...), custom_call_target="tpu_custom_call", output_to_operand_aliasing={{1}: (8, {}), {2}: (9, {}), {3}: (10, {}), {4}: (11, {}), {... | custom-call | tf_op jit(solution)/shard_map/while/body/eval_jaxpr/pallas_call | solution.py:316
  200.9 1.9 copy.113
  202.8 1.9 copy.106
  204.7 1.9 collective-permute-start
  207.4 12.3 %eval_jaxpr.5 = (bf16[128,2048]{1,0:T(8,128)(2,1)}, bf16[4,128,2048]{2,1,0:T(8,128)(2,1)}, bf16[4,128,1024]{2,1,0:T(8,128)(2,1)}, bf16[4,128,1024]{2,1,0:T(8,128...) custom-call(s32[7]{0:T(128)} %pad_add_fusion.2.scal, ...), custom_call_target="tpu_custom_call", output_to_operand_aliasing={{1}: (8, {}), {2}: (9, {}), {3}: (10, {}), {4}: (11, {}), {... | custom-call | tf_op jit(solution)/shard_map/while/body/eval_jaxpr/pallas_call | solution.py:316
  219.8 1.9 copy.113
  221.6 1.9 copy.106
  223.6 1.9 collective-permute-start
  226.3 12.3 %eval_jaxpr.5 = (bf16[128,2048]{1,0:T(8,128)(2,1)}, bf16[4,128,2048]{2,1,0:T(8,128)(2,1)}, bf16[4,128,1024]{2,1,0:T(8,128)(2,1)}, bf16[4,128,1024]{2,1,0:T(8,128...) custom-call(s32[7]{0:T(128)} %pad_add_fusion.2.scal, ...), custom_call_target="tpu_custom_call", output_to_operand_aliasing={{1}: (8, {}), {2}: (9, {}), {3}: (10, {}), {4}: (11, {}), {... | custom-call | tf_op jit(solution)/shard_map/while/body/eval_jaxpr/pallas_call | solution.py:316
  238.6 1.9 copy.113
  240.5 1.9 copy.106
  242.4 1.9 collective-permute-start
  245.1 12.3 %eval_jaxpr.5 = (bf16[128,2048]{1,0:T(8,128)(2,1)}, bf16[4,128,2048]{2,1,0:T(8,128)(2,1)}, bf16[4,128,1024]{2,1,0:T(8,128)(2,1)}, bf16[4,128,1024]{2,1,0:T(8,128...) custom-call(s32[7]{0:T(128)} %pad_add_fusion.2.scal, ...), custom_call_target="tpu_custom_call", output_to_operand_aliasing={{1}: (8, {}), {2}: (9, {}), {3}: (10, {}), {4}: (11, {}), {... | custom-call | tf_op jit(solution)/shard_map/while/body/eval_jaxpr/pallas_call | solution.py:316
  257.5 1.9 copy.113
  259.4 1.9 copy.106
  261.3 1.9 collective-permute-start
  264.9 7.2 %collective-permute-done = bf16[128,2048]{1,0:T(8,128)(2,1)} collective-permute-done((bf16[128,2048]{1,0:T(8,128)(2,1)}, bf16[128,2048]{1,0:T(8,128)(2,1)}, u32[]{:S(2)}, u32[]{:S(2)}) %collective-permute-start) | collective-permute-done | bytes 524320 | tf_op jit(solution)/shard_map/while/body/eval_jaxpr/ppermute | solution.py:310
  272.1 1.9 copy.113
  274.0 1.9 copy.106
  275.9 1.9 collective-permute-start
  279.5 7.2 %collective-permute-done = bf16[128,2048]{1,0:T(8,128)(2,1)} collective-permute-done((bf16[128,2048]{1,0:T(8,128)(2,1)}, bf16[128,2048]{1,0:T(8,128)(2,1)}, u32[]{:S(2)}, u32[]{:S(2)}) %collective-permute-start) | collective-permute-done | bytes 524320 | tf_op jit(solution)/shard_map/while/body/eval_jaxpr/ppermute | solution.py:310
  286.7 1.9 copy.113
  288.6 3.8 convolution_bitcast_fusion.1
  292.4 2.5 convolution_bitcast_fusion
  295.0 4.8 fusion
  299.8 1.5 copy.85
  302.5 7.0 %all-to-all-start.2 = ((bf16[8,4,128,128]{3,2,1,0:T(8,128)(2,1)}), bf16[8,4,128,128]{3,2,1,0:T(8,128)(2,1)}, u32[]{:S(2)}, u32[]{:S(2)}) async-start(bf16[8,4,128,128]{3,2,1,0:T(8,128)(2,1)} %bitcast.81), calls=%async_computation.3 | async-start | bytes 2097152 | tf_op jit(solution)/shard_map/all_to_all | solution.py:241
  309.5 1.5 copy.86
  312.2 43.0 %all-to-all-done.2.q_ref = bf16[8,4,128,128]{3,2,1,0:T(8,128)(2,1)} async-done(((bf16[8,4,128,128]{3,2,1,0:T(8,128)(2,1)}), bf16[8,4,128,128]{3,2,1,0:T(8,128)(2,1)}, u32[]{:S(2)}, u32[]{:S(2)}) %all-to-all-start.2) | async-done | bytes 1048608 | tf_op jit(solution)/shard_map/all_to_all | solution.py:241
  355.2 10.9 %all-to-all-start.4 = ((bf16[8,2,2,128,128]{4,3,2,1,0:T(8,128)(2,1)}), bf16[8,2,2,128,128]{4,3,2,1,0:T(8,128)(2,1)}, u32[]{:S(2)}, u32[]{:S(2)}) async-start(bf16[8,2,2,128,128]{4,3,2,1,0:T(8,128)(2,1)} %bitcast.80), calls=%async_computation.5 | async-start | bytes 2097152 | tf_op jit(solution)/shard_map/all_to_all | solution.py:241
  367.4 2.3 copy.79
  369.7 40.6 %all-to-all-done.4 = bf16[8,2,2,128,128]{4,3,2,1,0:T(8,128)(2,1)} async-done(((bf16[8,2,2,128,128]{4,3,2,1,0:T(8,128)(2,1)}), bf16[8,2,2,128,128]{4,3,2,1,0:T(8,128)(2,1)}, u32[]{:S(2)}, u32[]{:S(2)}) %all-to-all-start.4) | async-done | bytes 1048608 | tf_op jit(solution)/shard_map/all_to_all | solution.py:241
  410.3 10.3 %all-to-all-start.3 = ((bf16[8,4,128,128]{3,2,1,0:T(8,128)(2,1)}), bf16[8,4,128,128]{3,2,1,0:T(8,128)(2,1)S(1)}, u32[]{:S(2)}, u32[]{:S(2)}) async-start(bf16[8,4,128,128]{3,2,1,0:T(8,128)(2,1)} %bitcast.79), calls=%async_computation.4 | async-start | bytes 2097152 | tf_op jit(solution)/shard_map/all_to_all | solution.py:241
  422.2 36.3 %all_gather.3 = s32[4,16,2]{0,2,1:T(2,128)S(1)} all-gather(s32[4,2,2]{0,2,1:T(2,128)S(1)} %copy-done.5), channel_id=1, replica_groups=mesh['section'=4,'dp'=8] {'dp'}, dimensions={1}, use_global_device_ids=true | all-gather | bytes 576 | tf_op jit(solution)/shard_map/all_gather | solution.py:350
  461.2 35.5 %shard_map.112 = bf16[16,2,128,128]{3,2,1,0:T(8,128)(2,1)} custom-call(s32[128]{0:T(128)} %reshape.85.ids, s32[128]{0:T(128)} %reshape.86.mask, bf16[8,4,128,128]{3,2,1,0:T(8,128)(2,1)} %all-to-all-done.2.q_ref, bf16[8,4,128,128]{3,2,1,0:T(8,128)(2,1)} %copy-done.4, bf16[16,2,128,128]{3,2,1,0:T(8,128)(2,1)} %bitcast.28.kv_ref), custom_call_target="tpu_custom_call" | custom-call | tf_op jit(solution)/shard_map/pallas_call | solution.py:359
  496.7 27.9 %all_to_all.31 = bf16[8,2,2,128,128]{4,3,2,1,0:T(8,128)(2,1)S(1)} all-to-all(bf16[8,2,2,128,128]{4,3,2,1,0:T(8,128)(2,1)} %bitcast.76), channel_id=1, replica_groups=mesh['section'=4,'dp'=8] {'dp'}, dimensions={0} | all-to-all | bytes 2097152 | tf_op jit(solution)/shard_map/all_to_all | solution.py:241
  (95 shorter events, 30.9 us)
Async XLA Ops:
  7.2 61.5 %copy-start = (bf16[1,4,128,2048]{3,2,1,0:T(8,128)(2,1)S(1)}, bf16[1,4,128,2048]{3,2,1,0:T(8,128)(2,1)}, u32[]{:S(2)}) copy-start(bf16[1,4,128,2048]{3,2,1,0:T(8,128)(2,1)} %param.12) | copy-start | bytes 6291460
  7.2 1.4 copy-start.7
  7.2 1.4 copy-start.6
  62.6 5.4 %copy-start.5 = (s32[4,2,2]{0,2,1:T(2,128)S(1)}, s32[4,2,2]{0,2,1:T(2,128)}, u32[]{:S(2)}) copy-start(s32[4,2,2]{0,2,1:T(2,128)} %param.17) | copy-start | bytes 196
  62.6 51.3 %all-to-all-start.1 = ((bf16[8,128,1024]{2,1,0:T(8,128)(2,1)}), bf16[8,128,1024]{2,1,0:T(8,128)(2,1)}, u32[]{:S(2)}, u32[]{:S(2)}) async-start(bf16[8,128,1024]{2,1,0:T(8,128)(2,1)} %get-tuple-element.336), calls=%async_computation.1 | async-start | bytes 4194304 | tf_op jit(solution)/shard_map/all_to_all | solution.py:241
  67.9 458.6 %reduce-scatter.2.cloned.1.call-start = ((), (), s32[]{:S(2)}) async-start(), calls=%async_computation.7 | async-start | bytes 9437184 | tf_op jit(solution)/shard_map/reduce_scatter | solution.py:335
  68.7 5.6 %copy-start.1 = (bf16[8,128,1024]{2,1,0:T(8,128)(2,1)S(1)}, bf16[8,128,1024]{2,1,0:T(8,128)(2,1)}, u32[]{:S(2)}) copy-start(bf16[8,128,1024]{2,1,0:T(8,128)(2,1)} %all_to_all.30.k_ref) | copy-start | bytes 6291460
  123.1 10.8 %collective-permute-start = (bf16[128,2048]{1,0:T(8,128)(2,1)}, bf16[128,2048]{1,0:T(8,128)(2,1)}, u32[]{:S(2)}, u32[]{:S(2)}) collective-permute-start(bf16[128,2048]{1,0:T(8,128)(2,1)} %copy.106), channel_id=1, source_target_pairs={{8,0},{16,8},{24,16},{9,1},{17,9},{25,17},{10,2},{18,10},{26,18},{... | collective-permute-start | bytes 1572872 | tf_op jit(solution)/shard_map/while/body/eval_jaxpr/ppermute | solution.py:310
  137.7 10.8 %collective-permute-start = (bf16[128,2048]{1,0:T(8,128)(2,1)}, bf16[128,2048]{1,0:T(8,128)(2,1)}, u32[]{:S(2)}, u32[]{:S(2)}) collective-permute-start(bf16[128,2048]{1,0:T(8,128)(2,1)} %copy.106), channel_id=1, source_target_pairs={{8,0},{16,8},{24,16},{9,1},{17,9},{25,17},{10,2},{18,10},{26,18},{... | collective-permute-start | bytes 1572872 | tf_op jit(solution)/shard_map/while/body/eval_jaxpr/ppermute | solution.py:310
  152.3 10.8 %collective-permute-start = (bf16[128,2048]{1,0:T(8,128)(2,1)}, bf16[128,2048]{1,0:T(8,128)(2,1)}, u32[]{:S(2)}, u32[]{:S(2)}) collective-permute-start(bf16[128,2048]{1,0:T(8,128)(2,1)} %copy.106), channel_id=1, source_target_pairs={{8,0},{16,8},{24,16},{9,1},{17,9},{25,17},{10,2},{18,10},{26,18},{... | collective-permute-start | bytes 1572872 | tf_op jit(solution)/shard_map/while/body/eval_jaxpr/ppermute | solution.py:310
  167.0 15.1 %collective-permute-start = (bf16[128,2048]{1,0:T(8,128)(2,1)}, bf16[128,2048]{1,0:T(8,128)(2,1)}, u32[]{:S(2)}, u32[]{:S(2)}) collective-permute-start(bf16[128,2048]{1,0:T(8,128)(2,1)} %copy.106), channel_id=1, source_target_pairs={{8,0},{16,8},{24,16},{9,1},{17,9},{25,17},{10,2},{18,10},{26,18},{... | collective-permute-start | bytes 1572872 | tf_op jit(solution)/shard_map/while/body/eval_jaxpr/ppermute | solution.py:310
  185.8 15.1 %collective-permute-start = (bf16[128,2048]{1,0:T(8,128)(2,1)}, bf16[128,2048]{1,0:T(8,128)(2,1)}, u32[]{:S(2)}, u32[]{:S(2)}) collective-permute-start(bf16[128,2048]{1,0:T(8,128)(2,1)} %copy.106), channel_id=1, source_target_pairs={{8,0},{16,8},{24,16},{9,1},{17,9},{25,17},{10,2},{18,10},{26,18},{... | collective-permute-start | bytes 1572872 | tf_op jit(solution)/shard_map/while/body/eval_jaxpr/ppermute | solution.py:310
  204.7 15.1 %collective-permute-start = (bf16[128,2048]{1,0:T(8,128)(2,1)}, bf16[128,2048]{1,0:T(8,128)(2,1)}, u32[]{:S(2)}, u32[]{:S(2)}) collective-permute-start(bf16[128,2048]{1,0:T(8,128)(2,1)} %copy.106), channel_id=1, source_target_pairs={{8,0},{16,8},{24,16},{9,1},{17,9},{25,17},{10,2},{18,10},{26,18},{... | collective-permute-start | bytes 1572872 | tf_op jit(solution)/shard_map/while/body/eval_jaxpr/ppermute | solution.py:310
  223.6 15.1 %collective-permute-start = (bf16[128,2048]{1,0:T(8,128)(2,1)}, bf16[128,2048]{1,0:T(8,128)(2,1)}, u32[]{:S(2)}, u32[]{:S(2)}) collective-permute-start(bf16[128,2048]{1,0:T(8,128)(2,1)} %copy.106), channel_id=1, source_target_pairs={{8,0},{16,8},{24,16},{9,1},{17,9},{25,17},{10,2},{18,10},{26,18},{... | collective-permute-start | bytes 1572872 | tf_op jit(solution)/shard_map/while/body/eval_jaxpr/ppermute | solution.py:310
  242.4 15.0 %collective-permute-start = (bf16[128,2048]{1,0:T(8,128)(2,1)}, bf16[128,2048]{1,0:T(8,128)(2,1)}, u32[]{:S(2)}, u32[]{:S(2)}) collective-permute-start(bf16[128,2048]{1,0:T(8,128)(2,1)} %copy.106), channel_id=1, source_target_pairs={{8,0},{16,8},{24,16},{9,1},{17,9},{25,17},{10,2},{18,10},{26,18},{... | collective-permute-start | bytes 1572872 | tf_op jit(solution)/shard_map/while/body/eval_jaxpr/ppermute | solution.py:310
  261.3 10.8 %collective-permute-start = (bf16[128,2048]{1,0:T(8,128)(2,1)}, bf16[128,2048]{1,0:T(8,128)(2,1)}, u32[]{:S(2)}, u32[]{:S(2)}) collective-permute-start(bf16[128,2048]{1,0:T(8,128)(2,1)} %copy.106), channel_id=1, source_target_pairs={{8,0},{16,8},{24,16},{9,1},{17,9},{25,17},{10,2},{18,10},{26,18},{... | collective-permute-start | bytes 1572872 | tf_op jit(solution)/shard_map/while/body/eval_jaxpr/ppermute | solution.py:310
  275.9 10.8 %collective-permute-start = (bf16[128,2048]{1,0:T(8,128)(2,1)}, bf16[128,2048]{1,0:T(8,128)(2,1)}, u32[]{:S(2)}, u32[]{:S(2)}) collective-permute-start(bf16[128,2048]{1,0:T(8,128)(2,1)} %copy.106), channel_id=1, source_target_pairs={{8,0},{16,8},{24,16},{9,1},{17,9},{25,17},{10,2},{18,10},{26,18},{... | collective-permute-start | bytes 1572872 | tf_op jit(solution)/shard_map/while/body/eval_jaxpr/ppermute | solution.py:310
  288.6 3.8 copy-start.2
  288.6 3.8 copy-start.3
  302.5 52.7 %all-to-all-start.2 = ((bf16[8,4,128,128]{3,2,1,0:T(8,128)(2,1)}), bf16[8,4,128,128]{3,2,1,0:T(8,128)(2,1)}, u32[]{:S(2)}, u32[]{:S(2)}) async-start(bf16[8,4,128,128]{3,2,1,0:T(8,128)(2,1)} %bitcast.81), calls=%async_computation.3 | async-start | bytes 2097152 | tf_op jit(solution)/shard_map/all_to_all | solution.py:241
  355.2 55.1 %all-to-all-start.4 = ((bf16[8,2,2,128,128]{4,3,2,1,0:T(8,128)(2,1)}), bf16[8,2,2,128,128]{4,3,2,1,0:T(8,128)(2,1)}, u32[]{:S(2)}, u32[]{:S(2)}) async-start(bf16[8,2,2,128,128]{4,3,2,1,0:T(8,128)(2,1)} %bitcast.80), calls=%async_computation.5 | async-start | bytes 2097152 | tf_op jit(solution)/shard_map/all_to_all | solution.py:241
  410.3 49.8 %all-to-all-start.3 = ((bf16[8,4,128,128]{3,2,1,0:T(8,128)(2,1)}), bf16[8,4,128,128]{3,2,1,0:T(8,128)(2,1)S(1)}, u32[]{:S(2)}, u32[]{:S(2)}) async-start(bf16[8,4,128,128]{3,2,1,0:T(8,128)(2,1)} %bitcast.79), calls=%async_computation.4 | async-start | bytes 2097152 | tf_op jit(solution)/shard_map/all_to_all | solution.py:241
  460.2 1.0 copy-start.4
Sparse Core Ops, SparseCore 0:
  299.9 204.4 reduce-scatter.1
